TPU v7x, 32 devices: a whole 2x2x4 slice. The times are simulated.
32 devices in a mesh: groups: 2 (over x), band: 16 (over z, y, core).
Axes of the slice: x: 2, y: 2, z: 4, core: 2. Of those that a mesh axis runs over, the one named last changes fastest.
Arguments:
- orbitals: bfloat16 [2560, 32, 128], P(('groups', 'band')), parts along dimension 0, may hold values from -24 to 24
- potential: float32 [64, 128], P('groups'), parts along dimension 0, may hold values from -2 to 0
- plan: int32 [4, 16], P('groups'), parts along dimension 0, may hold values from 0 to 15, as said below
- owners: int32 [4, 16], P('groups'), parts along dimension 0, may hold values from 0 to 15, each once within a row
Outputs:
- filtered: bfloat16 [2560, 32, 128], P(('groups', 'band')), parts along dimension 0
- tiles: float32 [2, 2560, 80], P(None, ('groups', 'band')), parts along dimension 1
There are 2 independent parts, one for each index of `groups`. A program takes and returns all parts, laid end to end along the dimension named above; each array names one. Nothing has to cross between parts.
Inputs may be any that keep to these rules, and one draw needn't show every extreme that they name: In each of the 2 rounds the band groups are paired by a round-robin tournament: plan[r, i] is never i and plan[r, plan[r, i]] = i. `owners`: each row is a permutation of the band groups.
All inputs are finite; a program needn't handle non-finite values.
Results may differ from a plain program's by a relative error of at most 0.0055.
Values may be sent and summed in bfloat16 or wider, within the bound.
A program may use at most 192 MiB of HBM per device.

v0:
```python
import math
import jax
import jax.numpy as jnp
from jax import lax
from jax.sharding import PartitionSpec as P

NZ = 16
ROUNDS = 2
lower_edge = -2.5
cutoff_edge = 4.0
upper_edge = 8.5
half_width = (upper_edge - cutoff_edge) / 2.0
middle_point = (upper_edge + cutoff_edge) / 2.0


def with_halo(array, sides, width):
    for axis, dim in sides:
        devices, length = (lax.axis_size(axis), array.shape[dim])
        up = [(i, (i + 1) % devices) for i in range(devices - 1)]
        down = [(j, i) for i, j in up]
        last = lax.slice_in_dim(array, length - width, length, axis=dim)
        leading = lax.slice_in_dim(array, 0, width, axis=dim)
        before = lax.ppermute(last, axis, up)
        after = lax.ppermute(leading, axis, down)
        array = jnp.concatenate([before, array, after], axis=dim)
    return array


def chebyshev_filter(start_values, operator):
    sigma_zero = half_width / (lower_edge - middle_point)
    previous = start_values
    current = sigma_zero / half_width * (operator(start_values) - middle_point * start_values)
    sigma_now = sigma_zero
    sigma_next = 1.0 / (2.0 / sigma_zero - sigma_now)
    following = (
        2.0 * sigma_next / half_width * (operator(current) - middle_point * current)
        - sigma_now * sigma_next * previous
    )
    previous, current, sigma_now = (current, following, sigma_next)
    return current


def plane_part(center):
    span = center.shape[-1]
    margin = 2 * NZ
    padded = jnp.pad(center, ((0, 0), (0, 0), (margin, margin)))
    z_pos = jnp.arange(span, dtype=jnp.int32) % NZ

    def moved(offset):
        return lax.slice_in_dim(padded, margin + offset, margin + offset + span, axis=2)

    def z_term(offset):
        inside = ((z_pos + offset >= 0) & (z_pos + offset < NZ)).astype(jnp.float32)
        return moved(offset) * inside

    along_z = (
        -2.5 * center + 4.0 / 3.0 * (z_term(1) + z_term(-1)) - 1.0 / 12.0 * (z_term(2) + z_term(-2))
    )
    along_y = (
        -2.5 * center
        + 4.0 / 3.0 * (moved(NZ) + moved(-NZ))
        - 1.0 / 12.0 * (moved(2 * NZ) + moved(-2 * NZ))
    )
    return -0.5 * (along_y + along_z)


def energy(center, plus_one, minus_one, plus_two, minus_two, local_pot):
    along_x = -0.5 * (
        -2.5 * center + 4.0 / 3.0 * (plus_one + minus_one) - 1.0 / 12.0 * (plus_two + minus_two)
    )
    return local_pot * center + along_x + plane_part(center)


def on_device(orbitals, potential, plan, owners):
    band_width = orbitals.shape[0]
    group_count = lax.axis_size("band")
    planes = orbitals.shape[1] // group_count
    norm_factor = 1.0 / math.sqrt(orbitals.shape[1] * orbitals.shape[2])

    def whole_apply(values):
        length = values.shape[1]
        padded = jnp.pad(values, ((0, 0), (2, 2), (0, 0)))
        return energy(
            values,
            padded[:, 3 : 3 + length],
            padded[:, 1 : 1 + length],
            padded[:, 4 : 4 + length],
            padded[:, 0:length],
            potential,
        )

    filtered = chebyshev_filter(orbitals.astype(jnp.float32), whole_apply).astype(jnp.bfloat16)
    slab_orbitals = lax.all_to_all(filtered, "band", split_axis=1, concat_axis=0, tiled=True)
    padded = with_halo(slab_orbitals, (("band", 1),), 2).astype(jnp.float32)
    slab_pot = lax.dynamic_slice_in_dim(potential, lax.axis_index("band") * planes, planes, 0)
    slab_applied = energy(
        padded[:, 2 : 2 + planes],
        padded[:, 3 : 3 + planes],
        padded[:, 1 : 1 + planes],
        padded[:, 4 : 4 + planes],
        padded[:, 0:planes],
        slab_pot,
    ).astype(jnp.bfloat16)
    orbital_groups = slab_orbitals.reshape(group_count, band_width, -1)
    applied_groups = slab_applied.reshape(group_count, band_width, -1)
    collected = []
    for round_index in range(ROUNDS):
        inverse = jnp.argsort(owners[round_index])
        partner = plan[round_index]
        left_block = jnp.take(orbital_groups, inverse, axis=0)
        right_block = jnp.take(applied_groups, jnp.take(partner, inverse), axis=0)
        product = jnp.einsum(
            "kac,kbc->kab", left_block, right_block, preferred_element_type=jnp.float32
        )
        collected.append(
            lax.psum_scatter(
                (product * norm_factor).reshape(band_width * lax.axis_size("band"), band_width),
                "band",
                scatter_dimension=0,
                tiled=True,
            )
        )
    tiles = jnp.stack(collected)
    return (filtered, tiles)


def solution(mesh):
    placed = (
        P(("groups", "band"), None, None),
        P("groups", None),
        P("groups", None),
        P("groups", None),
    )
    return jax.shard_map(
        on_device,
        mesh=mesh,
        in_specs=placed,
        out_specs=(P(("groups", "band"), None, None), P(None, ("groups", "band"), None)),
        check_vma=False,
    )
```

profile of v0, /device:TPU:0, one launch (start us, length us, event | category | flops | bytes accessed | tf_op | source)
XLA Modules:
  0.0 194.6 jit_solution(11361527517866755214)
XLA Ops:
  7.2 0.0 copy-start.1
  7.2 1.3 copy_convert_fusion
  8.5 0.0 copy-done.1
  8.5 0.0 copy-start
  8.5 2.9 %broadcast_multiply_fusion = (f32[80,32,128]{2,0,1:T(8,128)S(1)}, f32[80,32,128]{2,0,1:T(8,128)S(1)}) fusion(f32[80,32,128]{2,0,1:T(8,128)S(1)} %copy_convert_fusion, f32[128]{0:T(128)S(1)} %get-tuple-element.22, f32[128]{0:T(128)S(1)} %get-tuple-element.23, f32[128]{0:T(128)S(1)} %get-tuple-element.24, f32[128]{0:T(128)S(1)} %get-tuple-element.25, ...), kind=kLoop, calls=%fused_computation.134 | loop fusion | flops 10485760 | bytes 3950592 | tf_op jit(solution)/shard_map/mul | solution.py:32
  11.4 0.0 copy-done
  11.5 3.7 %fusion.20 = bf16[80,32,128]{2,0,1:T(8,128)(2,1)} fusion(f32[80,32,128]{2,0,1:T(8,128)S(1)} %get-tuple-element.16, f32[80,32,128]{2,0,1:T(8,128)S(1)} %get-tuple-element.17, f32[32,128]{1,0:T(8,128)S(1)} %broadcast_multiply_fusion.1, f32[128]{0:T(128)S(1)} %get-tuple-element.22, f32[128]{0:T(128)S(1)} %get-tuple-element.23, f32[128]{0:T(128)S(1)} %get-tuple-element.24, ...), kind=kLoop, calls=%fused_computation.59 | loop fusion | flops 11796480 | bytes 3950592 | tf_op jit(solution)/shard_map/convert_element_type | solution.py:92
  15.2 0.0 copy-start.2
  15.2 0.0 copy-start.3
  15.2 7.5 %all-to-all-start = ((bf16[80,32,128]{2,0,1:T(8,128)(2,1)}), bf16[80,32,128]{2,0,1:T(8,128)(2,1)S(1)}, u32[]{:S(2)}, u32[]{:S(2)}) async-start(bf16[80,32,128]{2,0,1:T(8,128)(2,1)} %fusion.20), calls=%async_computation | async-start | bytes 1310720 | tf_op jit(solution)/shard_map/all_to_all | solution.py:93
  22.7 0.0 reduce-scatter.3.cloned.1.call-start
  22.8 0.0 copy-done.2
  22.8 1.2 sort.31
  24.1 0.0 copy-done.3
  24.1 0.7 gather_fusion.1
  24.8 1.3 sort.32
  26.0 13.3 %all-to-all-done = bf16[80,32,128]{2,0,1:T(8,128)(2,1)S(1)} async-done(((bf16[80,32,128]{2,0,1:T(8,128)(2,1)}), bf16[80,32,128]{2,0,1:T(8,128)(2,1)S(1)}, u32[]{:S(2)}, u32[]{:S(2)}) %all-to-all-start) | async-done | bytes 655392 | tf_op jit(solution)/shard_map/all_to_all | solution.py:93
  39.3 2.1 %collective-permute-start = (bf16[1280,2,128]{2,0,1:T(8,128)(2,1)S(1)}, bf16[1280,2,128]{2,0,1:T(8,128)(2,1)S(1)}, u32[]{:S(2)}, u32[]{:S(2)}) collective-permute-start(bf16[1280,2,128]{2,0,1:T(8,128)(2,1)S(1)} %bitcast.24), channel_id=1, source_target_pairs={{0,1},{1,2},{2,3},{3,4},{4,5},{5,6},{6,7},{7,8},{8,9},{9,10},{10,1... | collective-permute-start | bytes 1966088 | tf_op jit(solution)/shard_map/ppermute | solution.py:23
  41.5 1.3 collective-permute-start.1
  42.8 0.1 copy.17
  43.0 0.6 gather_fusion
  43.5 0.0 collective-permute-done
  43.6 2.1 %collective-permute-done.1 = bf16[1280,2,128]{2,0,1:T(8,128)(2,1)} collective-permute-done((bf16[1280,2,128]{2,0,1:T(8,128)(2,1)S(1)}, bf16[1280,2,128]{2,0,1:T(8,128)(2,1)}, u32[]{:S(2)}, u32[]{:S(2)}) %collective-permute-start.1) | collective-permute-done | bytes 655392 | tf_op jit(solution)/shard_map/ppermute | solution.py:24
  45.6 1.4 maximum_convert_fusion
  47.0 0.1 slice.176
  47.1 2.9 %fusion.66 = bf16[1280,2,128]{2,0,1:T(8,128)(2,1)S(1)} fusion(f32[1280,2,128]{2,0,1:T(8,128)S(1)} %slice.176, f32[1280,6,128]{2,0,1:T(8,128)S(1)} %maximum_convert_fusion, f32[128]{0:T(128)S(1)} %get-tuple-element.22, f32[128]{0:T(128)S(1)} %get-tuple-element.23, f32[128]{0:T(128)S(1)} %get-tuple-element.24, f32[128]{0:T(128)S(1)} %get-tuple-element.25, ...), kind=kLoop, calls=%fused_computation.105 | loop fusion | flops 9830400 | bytes 7212032 | tf_op jit(solution)/shard_map/convert_element_type | solution.py:103
  50.0 5.4 %copy.10 = bf16[1280,2,128]{2,1,0:T(2,128)(2,1)S(1)} copy(bf16[1280,2,128]{2,0,1:T(8,128)(2,1)S(1)} %fusion.66) | data formatting | bytes 1310720 | tf_op jit(solution)/shard_map/convert_element_type | solution.py:103
  55.5 0.4 reshape.65
  55.9 0.6 gather_fusion.2
  56.5 1.3 convolution_multiply_fusion.1
  57.8 0.0 reduce-scatter.3.cloned.1.call-update
  57.8 0.0 reduce-scatter.5.cloned.1.call-start
  57.8 0.7 gather_fusion.4
  58.5 0.6 gather_fusion.3
  59.1 0.6 gather_fusion.5
  59.7 1.3 convolution_multiply_fusion
  61.0 0.0 reduce-scatter.5.cloned.1.call-update
  61.0 2.1 %copy.11 = bf16[80,32,128]{2,1,0:T(8,128)(2,1)} copy(bf16[80,32,128]{2,0,1:T(8,128)(2,1)} %fusion.20) | data formatting | bytes 1310720
  63.1 64.1 %reduce-scatter.3.cloned.1.call-done = f32[80,80]{1,0:T(8,128)} async-done(((f32[1280,80]{1,0:T(8,128)}), f32[80,80]{1,0:T(8,128)}) %reduce-scatter.3.cloned.1.call-update) | async-done | bytes 25616 | tf_op jit(solution)/shard_map/reduce_scatter | solution.py:116
  127.2 59.1 %reduce-scatter.5.cloned.1.call-done = f32[80,80]{1,0:T(8,128)} async-done(((f32[1280,80]{1,0:T(8,128)}), f32[80,80]{1,0:T(8,128)}) %reduce-scatter.5.cloned.1.call-update) | async-done | bytes 25616 | tf_op jit(solution)/shard_map/reduce_scatter | solution.py:116
  186.3 1.4 pad_maximum_fusion
  (17 shorter events, 0.2 us)
Async XLA Ops:
  7.2 1.3 copy-start.1
  8.5 2.9 %copy-start = (bf16[80,32,128]{2,1,0:T(8,128)(2,1)S(1)}, bf16[80,32,128]{2,1,0:T(8,128)(2,1)}, u32[]{:S(2)}) copy-start(bf16[80,32,128]{2,1,0:T(8,128)(2,1)} %param.8) | copy-start | bytes 1966084
  15.2 7.6 %copy-start.2 = (s32[2,16]{1,0:T(2,128)S(1)}, s32[2,16]{1,0:T(2,128)}, u32[]{:S(2)}) copy-start(s32[2,16]{1,0:T(2,128)} %param.11) | copy-start | bytes 388
  15.2 8.9 %copy-start.3 = (s32[2,16]{1,0:T(2,128)S(1)}, s32[2,16]{1,0:T(2,128)}, u32[]{:S(2)}) copy-start(s32[2,16]{1,0:T(2,128)} %param.10) | copy-start | bytes 388
  15.2 24.1 %all-to-all-start = ((bf16[80,32,128]{2,0,1:T(8,128)(2,1)}), bf16[80,32,128]{2,0,1:T(8,128)(2,1)S(1)}, u32[]{:S(2)}, u32[]{:S(2)}) async-start(bf16[80,32,128]{2,0,1:T(8,128)(2,1)} %fusion.20), calls=%async_computation | async-start | bytes 1310720 | tf_op jit(solution)/shard_map/all_to_all | solution.py:93
  22.7 104.5 %reduce-scatter.3.cloned.1.call-start = ((), (), s32[]{:S(2)}) async-start(), calls=%async_computation.3 | async-start | bytes 696320 | tf_op jit(solution)/shard_map/reduce_scatter | solution.py:116
  39.3 4.2 %collective-permute-start = (bf16[1280,2,128]{2,0,1:T(8,128)(2,1)S(1)}, bf16[1280,2,128]{2,0,1:T(8,128)(2,1)S(1)}, u32[]{:S(2)}, u32[]{:S(2)}) collective-permute-start(bf16[1280,2,128]{2,0,1:T(8,128)(2,1)S(1)} %bitcast.24), channel_id=1, source_target_pairs={{0,1},{1,2},{2,3},{3,4},{4,5},{5,6},{6,7},{7,8},{8,9},{9,10},{10,1... | collective-permute-start | bytes 1966088 | tf_op jit(solution)/shard_map/ppermute | solution.py:23
  41.5 4.2 %collective-permute-start.1 = (bf16[1280,2,128]{2,0,1:T(8,128)(2,1)S(1)}, bf16[1280,2,128]{2,0,1:T(8,128)(2,1)}, u32[]{:S(2)}, u32[]{:S(2)}) collective-permute-start(bf16[1280,2,128]{2,0,1:T(8,128)(2,1)S(1)} %bitcast.25), channel_id=1, source_target_pairs={{1,0},{2,1},{3,2},{4,3},{5,4},{6,5},{7,6},{8,7},{9,8},{10,9},{11,1... | collective-permute-start | bytes 1966088 | tf_op jit(solution)/shard_map/ppermute | solution.py:24
  57.8 128.6 %reduce-scatter.5.cloned.1.call-start = ((), (), s32[]{:S(2)}) async-start(), calls=%async_computation.4 | async-start | bytes 696320 | tf_op jit(solution)/shard_map/reduce_scatter | solution.py:116
Sparse Core Ops, SparseCore 0:
  57.9 69.2 reduce-scatter.2
  130.7 55.5 reduce-scatter.4
where the time goes:
time: 195 us
  waiting for transfers between devices  139 us (71%)
  other arithmetic  16.2 us (8%)
  between operations  14.3 us (7%)
  local copies, waits for them, and re-layouts  11.9 us (6%)
  starting transfers between devices  11 us (6%)
  matrix products  2.55 us (1%)
    reduce_scatter x2, waiting for transfers between devices, on_device(): lax.psum_scatter((product * norm_factor).reshape(band_width * lax.axis_si...  123 us
    all_to_all x1, waiting for transfers between devices, on_device(): lax.all_to_all(filtered, 'band', split_axis=1, concat_axis=0, tiled=True)  13.3 us
    all_to_all x1, starting transfers between devices, on_device(): lax.all_to_all(filtered, 'band', split_axis=1, concat_axis=0, tiled=True)  7.55 us
    convert_element_type x1, local copies, waits for them, and re-layouts, on_device(): slab_applied = energy(padded[:, 2:2 + planes], padded[:, 3:3 + planes], p...  5.44 us
  transfers between devices with their start and end apart: 5, of which 4 were waited for; matrix products, arithmetic and copies ran while one was open for 5% of the time, Pallas kernels for 0%

commit v1 on v0

--- a/solution.py
+++ b/solution.py
@@ -11,6 +11,12 @@
 upper_edge = 8.5
 half_width = (upper_edge - cutoff_edge) / 2.0
 middle_point = (upper_edge + cutoff_edge) / 2.0
+
+
+def trade_parts(x, name, split, join):
+    pieces = jnp.split(x, lax.axis_size(name), axis=split)
+    got = lax.all_to_all(jnp.stack(pieces), name, 0, 0)
+    return jnp.concatenate(got, axis=join)
 
 
 def with_halo(array, sides, width):
@@ -90,7 +96,7 @@
         )
 
     filtered = chebyshev_filter(orbitals.astype(jnp.float32), whole_apply).astype(jnp.bfloat16)
-    slab_orbitals = lax.all_to_all(filtered, "band", split_axis=1, concat_axis=0, tiled=True)
+    slab_orbitals = trade_parts(filtered, "band", 1, 0)
     padded = with_halo(slab_orbitals, (("band", 1),), 2).astype(jnp.float32)
     slab_pot = lax.dynamic_slice_in_dim(potential, lax.axis_index("band") * planes, planes, 0)
     slab_applied = energy(

time: 195 us -> 205 us (1.051)
  local copies, waits for them, and re-layouts: 11.9 us -> 20.6 us
    unnamed x9 -> x25, local copies, waits for them, and re-layouts: 2.11 us -> 9.8 us
    reduce_scatter x2, waiting for transfers between devices: 123 us -> 126 us  [on_device(): lax.psum_scatter((product * norm_factor).reshape(band_width * lax.axis_si...]
  transfers between devices with their start and end apart: 5 -> 5, of which waited for: 4 -> 4; matrix products, arithmetic and copies ran while one was open for 5% -> 4% of each run, Pallas kernels for 0% -> 0%
where the time goes in v1:
time: 205 us; the launch traced here: 204 us
  waiting for transfers between devices  140 us (68%)
  local copies, waits for them, and re-layouts  20.6 us (10%)
  other arithmetic  15.4 us (8%)
  between operations  14.3 us (7%)
  starting transfers between devices  10.9 us (5%)
  matrix products  2.52 us (1%)
    reduce_scatter x2, waiting for transfers between devices, on_device(): lax.psum_scatter((product * norm_factor).reshape(band_width * lax.axis_si...  126 us
    all_to_all x1, waiting for transfers between devices, trade_parts(): got = lax.all_to_all(jnp.stack(pieces), name, 0, 0)  12.6 us
    unnamed x25, local copies, waits for them, and re-layouts  9.8 us
    all_to_all x1, starting transfers between devices, trade_parts(): got = lax.all_to_all(jnp.stack(pieces), name, 0, 0)  7.41 us
    convert_element_type x1, local copies, waits for them, and re-layouts, on_device(): slab_applied = energy(padded[:, 2:2 + planes], padded[:, 3:3 + planes], p...  5.44 us
  transfers between devices with their start and end apart: 5, of which 4 were waited for; matrix products, arithmetic and copies ran while one was open for 4% of the time, Pallas kernels for 0%

profile of v1, /device:TPU:0, one launch (start us, length us, event | category | flops | bytes accessed | tf_op | source)
XLA Modules:
  0.0 204.2 jit_solution(12963302146448391239)
XLA Ops:
  7.2 0.0 copy-start.2
  7.2 1.2 convert_element_type.72
  8.4 0.0 copy-done.2
  8.5 0.0 copy-start
  8.5 2.9 %broadcast_multiply_fusion = (f32[80,32,128]{2,1,0:T(8,128)S(1)}, f32[80,32,128]{2,1,0:T(8,128)S(1)}) fusion(f32[80,32,128]{2,1,0:T(8,128)S(1)} %convert_element_type.72, f32[128]{0:T(128)S(1)} %get-tuple-element.20, f32[128]{0:T(128)S(1)} %get-tuple-element.21, f32[128]{0:T(128)S(1)} %get-tuple-element.22, f32[128]{0:T(128)S(1)} %get-tuple-element.23, ...), kind=kLoop, calls=%fused_computation.132 | loop fusion | flops 10485760 | bytes 3950592 | tf_op jit(solution)/shard_map/mul | solution.py:38
  11.4 0.0 copy-done
  11.4 2.9 %fusion.20 = bf16[80,32,128]{2,1,0:T(8,128)(2,1)S(1)} fusion(f32[80,32,128]{2,1,0:T(8,128)S(1)} %get-tuple-element.14, f32[80,32,128]{2,1,0:T(8,128)S(1)} %get-tuple-element.15, f32[32,128]{1,0:T(8,128)S(1)} %broadcast_multiply_fusion.1, f32[128]{0:T(128)S(1)} %get-tuple-element.20, f32[128]{0:T(128)S(1)} %get-tuple-element.21, ...), kind=kLoop, calls=%fused_computation.59 | loop fusion | flops 11796480 | bytes 3950592 | tf_op jit(solution)/shard_map/convert_element_type | solution.py:98
  14.3 0.0 copy-start.1
  14.4 0.0 copy-start.3
  14.4 0.0 copy-start.4
  14.4 0.6 fusion.110
  15.0 0.7 fusion.109
  15.7 0.7 fusion.108
  16.3 0.7 fusion.107
  17.0 0.6 fusion.106
  17.6 0.7 fusion.105
  18.3 0.7 fusion.104
  18.9 0.7 fusion.103
  19.6 0.6 fusion.102
  20.2 0.7 fusion.101
  20.9 0.7 fusion.100
  21.5 0.7 fusion.99
  22.2 0.6 fusion.98
  22.8 0.7 fusion.97
  23.5 0.7 fusion.96
  24.2 0.6 fusion.95
  24.8 0.0 copy-done.1
  24.8 7.4 %all-to-all-start = ((bf16[16,80,2,128]{3,2,1,0:T(2,128)(2,1)}), bf16[16,80,2,128]{3,2,1,0:T(2,128)(2,1)S(1)}, u32[]{:S(2)}, u32[]{:S(2)}) async-start(bf16[16,80,2,128]{3,2,1,0:T(2,128)(2,1)} %fusion.95), calls=%async_computation | async-start | bytes 1310720 | tf_op jit(solution)/shard_map/all_to_all | solution.py:18
  32.2 0.0 reduce-scatter.3.cloned.1.call-start
  32.3 0.0 copy-done.3
  32.3 1.2 sort.32
  33.6 0.0 copy-done.4
  33.6 0.7 gather_fusion.4
  34.3 1.3 sort.31
  35.5 0.7 gather_fusion.1
  36.2 12.6 %all-to-all-done = bf16[16,80,2,128]{3,2,1,0:T(2,128)(2,1)S(1)} async-done(((bf16[16,80,2,128]{3,2,1,0:T(2,128)(2,1)}), bf16[16,80,2,128]{3,2,1,0:T(2,128)(2,1)S(1)}, u32[]{:S(2)}, u32[]{:S(2)}) %all-to-all-start) | async-done | bytes 655392 | tf_op jit(solution)/shard_map/all_to_all | solution.py:18
  48.8 0.1 copy.7
  48.9 2.1 %collective-permute-start = (bf16[1280,2,128]{2,0,1:T(8,128)(2,1)S(1)}, bf16[1280,2,128]{2,0,1:T(8,128)(2,1)S(1)}, u32[]{:S(2)}, u32[]{:S(2)}) collective-permute-start(bf16[1280,2,128]{2,0,1:T(8,128)(2,1)S(1)} %bitcast.77), channel_id=1, source_target_pairs={{0,1},{1,2},{2,3},{3,4},{4,5},{5,6},{6,7},{7,8},{8,9},{9,10},{10,1... | collective-permute-start | bytes 1966088 | tf_op jit(solution)/shard_map/ppermute | solution.py:29
  51.0 1.3 collective-permute-start.1
  52.4 0.4 reshape_reshape.3
  52.8 0.6 gather_fusion
  53.4 0.0 collective-permute-done
  53.4 1.8 collective-permute-done.1
  55.2 1.4 maximum_convert_fusion
  56.6 0.1 slice.176
  56.7 2.9 %fusion.66 = bf16[1280,2,128]{2,0,1:T(8,128)(2,1)S(1)} fusion(f32[1280,2,128]{2,0,1:T(8,128)S(1)} %slice.176, f32[1280,6,128]{2,0,1:T(8,128)S(1)} %maximum_convert_fusion, f32[128]{0:T(128)S(1)} %get-tuple-element.20, f32[128]{0:T(128)S(1)} %get-tuple-element.21, f32[128]{0:T(128)S(1)} %get-tuple-element.22, f32[128]{0:T(128)S(1)} %get-tuple-element.23, ...), kind=kLoop, calls=%fused_computation.105 | loop fusion | flops 9830400 | bytes 7212032 | tf_op jit(solution)/shard_map/convert_element_type | solution.py:109
  59.6 5.4 %copy.8 = bf16[1280,2,128]{2,1,0:T(2,128)(2,1)S(1)} copy(bf16[1280,2,128]{2,0,1:T(8,128)(2,1)S(1)} %fusion.66) | data formatting | bytes 1310720 | tf_op jit(solution)/shard_map/convert_element_type | solution.py:109
  65.0 0.4 reshape.64
  65.4 0.6 gather_fusion.2
  66.0 1.3 convolution_multiply_fusion.1
  67.3 0.0 reduce-scatter.3.cloned.1.call-update
  67.3 0.0 reduce-scatter.5.cloned.1.call-start
  67.4 0.6 gather_fusion.3
  68.0 0.6 gather_fusion.5
  68.6 1.3 convolution_multiply_fusion
  69.8 0.0 reduce-scatter.5.cloned.1.call-update
  69.9 66.9 %reduce-scatter.3.cloned.1.call-done = f32[80,80]{1,0:T(8,128)} async-done(((f32[1280,80]{1,0:T(8,128)}), f32[80,80]{1,0:T(8,128)}) %reduce-scatter.3.cloned.1.call-update) | async-done | bytes 25616 | tf_op jit(solution)/shard_map/reduce_scatter | solution.py:122
  136.7 59.1 %reduce-scatter.5.cloned.1.call-done = f32[80,80]{1,0:T(8,128)} async-done(((f32[1280,80]{1,0:T(8,128)}), f32[80,80]{1,0:T(8,128)}) %reduce-scatter.5.cloned.1.call-update) | async-done | bytes 25616 | tf_op jit(solution)/shard_map/reduce_scatter | solution.py:122
  195.9 1.4 pad_maximum_fusion
  (15 shorter events, 0.1 us)
Async XLA Ops:
  7.2 1.3 copy-start.2
  8.5 2.9 %copy-start = (bf16[80,32,128]{2,1,0:T(8,128)(2,1)S(1)}, bf16[80,32,128]{2,1,0:T(8,128)(2,1)}, u32[]{:S(2)}) copy-start(bf16[80,32,128]{2,1,0:T(8,128)(2,1)} %param.8) | copy-start | bytes 1966084
  14.3 10.5 %copy-start.1 = (bf16[80,32,128]{2,1,0:T(8,128)(2,1)}, bf16[80,32,128]{2,1,0:T(8,128)(2,1)S(1)}, u32[]{:S(2)}) copy-start(bf16[80,32,128]{2,1,0:T(8,128)(2,1)S(1)} %fusion.20) | copy-start | bytes 1966084
  14.4 17.9 %copy-start.3 = (s32[2,16]{1,0:T(2,128)S(1)}, s32[2,16]{1,0:T(2,128)}, u32[]{:S(2)}) copy-start(s32[2,16]{1,0:T(2,128)} %param.11) | copy-start | bytes 388
  14.4 19.2 %copy-start.4 = (s32[2,16]{1,0:T(2,128)S(1)}, s32[2,16]{1,0:T(2,128)}, u32[]{:S(2)}) copy-start(s32[2,16]{1,0:T(2,128)} %param.10) | copy-start | bytes 388
  24.8 24.0 %all-to-all-start = ((bf16[16,80,2,128]{3,2,1,0:T(2,128)(2,1)}), bf16[16,80,2,128]{3,2,1,0:T(2,128)(2,1)S(1)}, u32[]{:S(2)}, u32[]{:S(2)}) async-start(bf16[16,80,2,128]{3,2,1,0:T(2,128)(2,1)} %fusion.95), calls=%async_computation | async-start | bytes 1310720 | tf_op jit(solution)/shard_map/all_to_all | solution.py:18
  32.2 104.5 %reduce-scatter.3.cloned.1.call-start = ((), (), s32[]{:S(2)}) async-start(), calls=%async_computation.3 | async-start | bytes 696320 | tf_op jit(solution)/shard_map/reduce_scatter | solution.py:122
  48.9 4.5 %collective-permute-start = (bf16[1280,2,128]{2,0,1:T(8,128)(2,1)S(1)}, bf16[1280,2,128]{2,0,1:T(8,128)(2,1)S(1)}, u32[]{:S(2)}, u32[]{:S(2)}) collective-permute-start(bf16[1280,2,128]{2,0,1:T(8,128)(2,1)S(1)} %bitcast.77), channel_id=1, source_target_pairs={{0,1},{1,2},{2,3},{3,4},{4,5},{5,6},{6,7},{7,8},{8,9},{9,10},{10,1... | collective-permute-start | bytes 1966088 | tf_op jit(solution)/shard_map/ppermute | solution.py:29
  51.0 4.2 %collective-permute-start.1 = (bf16[1280,2,128]{2,0,1:T(8,128)(2,1)S(1)}, bf16[1280,2,128]{2,0,1:T(8,128)(2,1)}, u32[]{:S(2)}, u32[]{:S(2)}) collective-permute-start(bf16[1280,2,128]{2,0,1:T(8,128)(2,1)S(1)} %bitcast.78), channel_id=1, source_target_pairs={{1,0},{2,1},{3,2},{4,3},{5,4},{6,5},{7,6},{8,7},{9,8},{10,9},{11,1... | collective-permute-start | bytes 1966088 | tf_op jit(solution)/shard_map/ppermute | solution.py:30
  67.3 128.6 %reduce-scatter.5.cloned.1.call-start = ((), (), s32[]{:S(2)}) async-start(), calls=%async_computation.4 | async-start | bytes 696320 | tf_op jit(solution)/shard_map/reduce_scatter | solution.py:122
Sparse Core Ops, SparseCore 0:
  67.4 69.2 reduce-scatter.2
  140.3 55.5 reduce-scatter.4
